TPU v7x, 32 devices: a whole 2x2x4 slice. The times are simulated.
32 devices in a mesh: ep: 16 (over z, y, core), rep: 2 (over x).
Axes of the slice: x: 2, y: 2, z: 4, core: 2. Of those that a mesh axis runs over, the one named last changes fastest.
Arguments:
- out_grad: bfloat16 [4096, 2048], P(('ep', 'rep')), may hold values from -6 to 6
- hidden: bfloat16 [4096, 8, 768], P(('ep', 'rep')), may hold values from -6 to 6
- expert_ids: int32 [4096, 8], P(('ep', 'rep')), may hold values from 0 to 15, all different within a row; in each aligned block of 128 rows (0 to 127, 128 to 255, ...) at most 72 rows name the same one
- gates: float32 [4096, 8], P(('ep', 'rep')), may hold values from 0.02 to 0.5
- weights: bfloat16 [16, 768, 2048], P('ep', 'rep'), may hold values from -0.125 to 0.125
- row_moment: float32 [16, 768], P('ep', 'rep'), may hold values from 16 to 1024
- col_moment: float32 [16, 2, 2048], P('ep', 'rep'), may hold values from 16 to 1024
Outputs:
- hidden_grad: bfloat16 [4096, 8, 768], P(('ep', 'rep'))
- update: bfloat16 [16, 768, 2048], P('ep', 'rep')
- row_new: float32 [16, 768], P('ep', 'rep')
- col_new: float32 [16, 2, 2048], P('ep', 'rep')
Inputs may be any that keep to these rules, and one draw needn't show every extreme that they name: `expert_ids`: the 8 experts of a token are distinct. Among the tokens of one device no expert is chosen more than 72 times, and in every draw some device reaches 72 for some expert.
All inputs are finite; a program needn't handle non-finite values.
Results may differ from a plain program's by a relative error of at most 0.014.
Values may be sent and summed in bfloat16 or wider, within the bound.
A program may use at most 128 MiB of HBM per device.

v0:
```python
import jax
import jax.numpy as jnp
from jax import lax
from jax.sharding import PartitionSpec as P

decay_rate = 0.9
epsilon = 1e-06


def local(out_grad, hidden, expert_ids, gates, weights, row_moment, col_moment):
    tok_rows, route_count = expert_ids.shape
    width = out_grad.shape[1]
    inner = hidden.shape[2]
    experts = lax.axis_size("ep")
    capacity = max(2, tok_rows * route_count * 9 // (8 * experts))
    routes = tok_rows * route_count
    flat_ids = expert_ids.reshape(routes)
    one_hot = (flat_ids[:, None] == jnp.arange(experts, dtype=jnp.int32)[None, :]).astype(jnp.int32)
    ranks = jnp.cumsum(one_hot, axis=0) - one_hot
    rank_own = jnp.sum(ranks * one_hot, axis=1)
    position = flat_ids * capacity + rank_own
    scaled = (
        (gates[:, :, None] * out_grad[:, None, :].astype(jnp.float32))
        .astype(jnp.bfloat16)
        .reshape(routes, width)
    )
    slots = experts * capacity
    send_scaled = jnp.zeros((slots, width), jnp.bfloat16).at[position].set(scaled)
    send_hidden = (
        jnp.zeros((slots, inner), jnp.bfloat16).at[position].set(hidden.reshape(routes, inner))
    )
    recv_scaled, recv_hidden = (
        lax.all_to_all(send_scaled, "ep", split_axis=0, concat_axis=0, tiled=True),
        lax.all_to_all(send_hidden, "ep", split_axis=0, concat_axis=0, tiled=True),
    )
    own_block = weights[0]
    input_grad = lax.dot_general(
        recv_scaled,
        lax.all_gather(own_block, "rep", axis=0, tiled=True),
        (((1,), (1,)), ((), ())),
        preferred_element_type=jnp.float32,
    ).astype(jnp.bfloat16)
    term = lax.dot_general(
        recv_hidden, recv_scaled, (((0,), (0,)), ((), ())), preferred_element_type=jnp.float32
    )
    gradient = lax.psum_scatter(
        lax.optimization_barrier(term.astype(jnp.bfloat16))
        .astype(jnp.float32)
        .astype(jnp.bfloat16),
        "rep",
        scatter_dimension=0,
        tiled=True,
    ).astype(jnp.float32)
    returned = lax.all_to_all(input_grad, "ep", split_axis=0, concat_axis=0, tiled=True)
    hidden_grad = returned[position].reshape(tok_rows, route_count, inner)
    squares = gradient * gradient
    row_new = decay_rate * row_moment[0] + (1.0 - decay_rate) * (
        jnp.mean(squares, axis=1) + epsilon
    )
    col_new = decay_rate * col_moment[0, 0] + (1.0 - decay_rate) * (
        jnp.mean(squares, axis=0) + epsilon
    )
    second = row_new[:, None] * col_new[None, :] / jnp.mean(row_new)
    update = (gradient * lax.rsqrt(second)).astype(jnp.bfloat16)
    return (hidden_grad, update[None], row_new[None], col_new[None, None])


def solution(mesh):
    return jax.shard_map(
        local,
        mesh=mesh,
        in_specs=(
            P(("ep", "rep"), None),
            P(("ep", "rep"), None, None),
            P(("ep", "rep"), None),
            P(("ep", "rep"), None),
            P("ep", "rep", None),
            P("ep", "rep"),
            P("ep", "rep", None),
        ),
        out_specs=(
            P(("ep", "rep"), None, None),
            P("ep", "rep", None),
            P("ep", "rep"),
            P("ep", "rep", None),
        ),
        check_vma=False,
    )
```

profile of v0, /device:TPU:15, one launch (start us, length us, event | category | flops | bytes accessed | tf_op | source)
XLA Modules:
  0.0 258.6 jit_solution(4397358027282598844)
XLA Ops:
  7.2 0.0 copy-start
  7.2 0.8 broadcast_multiply_fusion.1
  8.0 0.8 copy.14
  8.8 0.1 eq.29
  8.9 0.1 eq.25
  9.0 0.1 copy.13
  9.1 0.1 mul.126
  9.2 4.5 %reduce-window.6 = s32[16,8,128]{2,1,0:T(8,128)S(1)} reduce-window(s32[16,8,128]{2,1,0:T(8,128)S(1)} %fusion.17, s32[]{:T(128)} %constant.12.clone.1), window={size=1x1x128 pad=0_0x0_0x127_0}, to_apply=%region_0.0 | reduce-window | flops 2080768 | bytes 131076 | tf_op jit(solution)/shard_map/reduce-window
  13.7 0.1 slice.10
  13.8 0.1 copy.16
  13.9 0.1 copy.17
  14.0 0.1 broadcast_add_fusion
  14.2 0.0 copy-done
  14.2 0.0 copy-start.1
  14.2 6.6 %scatter_custom_fusion.1 = bf16[1152,768]{1,0:T(8,128)(2,1)} fusion(s32[1024]{0:T(1024)S(1)} %bitcast.55, bf16[128,8,768]{2,1,0:T(8,128)(2,1)S(1)} %copy-done, bf16[]{:T(256)} %constant.10.clone.1), kind=kCustom, calls=%fused_computation.18 | custom fusion | bytes 3342338 | tf_op jit(solution)/shard_map/scatter | solution.py:30
  20.7 0.0 copy-start.4
  20.7 6.7 %all-to-all-start.2 = ((bf16[16,72,768]{2,1,0:T(8,128)(2,1)}), bf16[16,72,768]{2,1,0:T(8,128)(2,1)}, u32[]{:S(2)}, u32[]{:S(2)}) async-start(bf16[16,72,768]{2,1,0:T(8,128)(2,1)} %bitcast.12), calls=%async_computation.2 | async-start | bytes 3538944 | tf_op jit(solution)/shard_map/all_to_all | solution.py:34
  27.4 0.0 copy-done.1
  27.4 0.1 convert_element_type.31
  27.5 0.0 copy-done.4
  27.5 0.1 copy.18
  27.6 0.1 mul.128
  27.7 9.8 %scatter_custom_fusion = bf16[1152,2048]{1,0:T(8,128)(2,1)} fusion(s32[1024]{0:T(1024)S(1)} %bitcast.56, f32[128,2048]{1,0:T(8,128)S(1)} %convert_element_type.31, f32[1024]{0:T(1024)S(1)} %mul.128, bf16[]{:T(256)} %constant.10.clone.1), kind=kCustom, calls=%fused_computation.6 | custom fusion | flops 4194304 | bytes 5771266 | tf_op jit(solution)/shard_map/scatter | solution.py:28
  37.5 30.4 %all-to-all-done.2 = bf16[16,72,768]{2,1,0:T(8,128)(2,1)} async-done(((bf16[16,72,768]{2,1,0:T(8,128)(2,1)}), bf16[16,72,768]{2,1,0:T(8,128)(2,1)}, u32[]{:S(2)}, u32[]{:S(2)}) %all-to-all-start.2) | async-done | bytes 1769504 | tf_op jit(solution)/shard_map/all_to_all | solution.py:34
  67.9 4.8 %all-to-all-start = ((bf16[16,72,2048]{2,1,0:T(8,128)(2,1)}), bf16[16,72,2048]{2,1,0:T(8,128)(2,1)}, u32[]{:S(2)}, u32[]{:S(2)}) async-start(bf16[16,72,2048]{2,1,0:T(8,128)(2,1)} %bitcast.47), calls=%async_computation | async-start | bytes 9437184 | tf_op jit(solution)/shard_map/all_to_all | solution.py:33
  72.7 0.0 all-gather.3.cloned.1.call-start
  72.7 0.7 all-gather.3.cloned.1.call-update
  73.4 0.2 reduce-scatter.2.cloned.1.call-start
  73.6 102.7 %all-to-all-done = bf16[16,72,2048]{2,1,0:T(8,128)(2,1)} async-done(((bf16[16,72,2048]{2,1,0:T(8,128)(2,1)}), bf16[16,72,2048]{2,1,0:T(8,128)(2,1)}, u32[]{:S(2)}, u32[]{:S(2)}) %all-to-all-start) | async-done | bytes 4718624 | tf_op jit(solution)/shard_map/all_to_all | solution.py:33
  176.4 8.8 %bitcast_convert_fusion = bf16[768,2048]{1,0:T(8,128)(2,1)} fusion(bf16[16,72,768]{2,1,0:T(8,128)(2,1)} %all-to-all-done.2, bf16[16,72,2048]{2,1,0:T(8,128)(2,1)} %all-to-all-done), kind=kOutput, calls=%fused_computation.5 | convolution fusion | flops 3625451520 | bytes 9633792 | tf_op jit(solution)/shard_map/dot_general | solution.py:43
  185.2 0.0 reduce-scatter.2.cloned.1.call-update
  185.2 0.0 all-gather.3.cloned.1.call-done
  185.3 8.4 %convolution_convert_fusion = bf16[1152,768]{1,0:T(8,128)(2,1)} fusion(bf16[1152,2048]{1,0:T(8,128)(2,1)} %bitcast.6, bf16[1,768,2048]{2,1,0:T(8,128)(2,1)} %all-gather.3.cloned.1.call-done), kind=kOutput, calls=%fused_computation.13 | convolution fusion | flops 3624763392 | bytes 9633792 | tf_op jit(solution)/shard_map/dot_general | solution.py:37
  193.7 0.0 copy-start.3
  193.7 4.9 %all-to-all-start.1 = ((bf16[16,72,768]{2,1,0:T(8,128)(2,1)}), bf16[16,72,768]{2,1,0:T(8,128)(2,1)S(1)}, u32[]{:S(2)}, u32[]{:S(2)}) async-start(bf16[16,72,768]{2,1,0:T(8,128)(2,1)} %bitcast.48), calls=%async_computation.1 | async-start | bytes 3538944 | tf_op jit(solution)/shard_map/all_to_all | solution.py:54
  198.6 0.0 copy-done.3
  198.7 40.4 %all-to-all-done.1 = bf16[16,72,768]{2,1,0:T(8,128)(2,1)S(1)} async-done(((bf16[16,72,768]{2,1,0:T(8,128)(2,1)}), bf16[16,72,768]{2,1,0:T(8,128)(2,1)S(1)}, u32[]{:S(2)}, u32[]{:S(2)}) %all-to-all-start.1) | async-done | bytes 1769504 | tf_op jit(solution)/shard_map/all_to_all | solution.py:54
  239.0 0.0 copy-start.2
  239.0 5.2 %gather_fusion = bf16[1024,768]{1,0:T(8,128)(2,1)} fusion(bf16[1152,768]{1,0:T(8,128)(2,1)S(1)} %bitcast.46, s32[1024]{0:T(1024)S(1)} %broadcast_clamp_fusion), kind=kCustom, calls=%fused_computation | custom fusion | bytes 3149824 | tf_op jit(solution)/shard_map/gather | solution.py:55
  244.2 0.0 reduce-scatter.2.cloned.1.call-done
  244.2 1.9 fusion.5
  246.1 0.0 copy-done.2
  246.1 0.6 fusion.20
  246.8 0.6 fusion.21
  247.4 0.6 reshape_add_fusion
  248.6 3.2 %fusion.10 = bf16[1,384,2048]{2,1,0:T(8,128)(2,1)} fusion(bf16[384,2048]{1,0:T(8,128)(2,1)} %reduce-scatter.2.cloned.1.call-done, f32[]{:T(128)S(6)} %div.25, f32[2048]{0:T(1024)S(1)} %fusion.19, f32[384]{0:T(512)S(1)} %get-tuple-element.7), kind=kLoop, calls=%fused_computation.17 | loop fusion | flops 3932160 | bytes 3155460 | tf_op jit(solution)/shard_map/broadcast_in_dim | solution.py:65
  (9 shorter events, 0.1 us)
Async XLA Ops:
  7.2 7.0 %copy-start = (bf16[128,8,768]{2,1,0:T(8,128)(2,1)S(1)}, bf16[128,8,768]{2,1,0:T(8,128)(2,1)}, u32[]{:S(2)}) copy-start(bf16[128,8,768]{2,1,0:T(8,128)(2,1)} %param.8) | copy-start | bytes 4718596
  14.2 13.2 %copy-start.1 = (bf16[128,2048]{1,0:T(8,128)(2,1)S(1)}, bf16[128,2048]{1,0:T(8,128)(2,1)}, u32[]{:S(2)}) copy-start(bf16[128,2048]{1,0:T(8,128)(2,1)} %param.7) | copy-start | bytes 1572868
  20.7 6.8 %copy-start.4 = (f32[128,8]{0,1:T(8,128)S(1)}, f32[128,8]{0,1:T(8,128)}, u32[]{:S(2)}) copy-start(f32[128,8]{0,1:T(8,128)} %param.10) | copy-start | bytes 12292
  20.7 47.2 %all-to-all-start.2 = ((bf16[16,72,768]{2,1,0:T(8,128)(2,1)}), bf16[16,72,768]{2,1,0:T(8,128)(2,1)}, u32[]{:S(2)}, u32[]{:S(2)}) async-start(bf16[16,72,768]{2,1,0:T(8,128)(2,1)} %bitcast.12), calls=%async_computation.2 | async-start | bytes 3538944 | tf_op jit(solution)/shard_map/all_to_all | solution.py:34
  67.9 108.5 %all-to-all-start = ((bf16[16,72,2048]{2,1,0:T(8,128)(2,1)}), bf16[16,72,2048]{2,1,0:T(8,128)(2,1)}, u32[]{:S(2)}, u32[]{:S(2)}) async-start(bf16[16,72,2048]{2,1,0:T(8,128)(2,1)} %bitcast.47), calls=%async_computation | async-start | bytes 9437184 | tf_op jit(solution)/shard_map/all_to_all | solution.py:33
  72.7 112.6 %all-gather.3.cloned.1.call-start = ((), (), s32[]{:S(2)}) async-start(), calls=%async_computation.5 | async-start | bytes 4718592 | tf_op jit(solution)/shard_map/all_gather | solution.py:39
  73.4 170.8 %reduce-scatter.2.cloned.1.call-start = ((), (), s32[]{:S(2)}) async-start(), calls=%async_computation.4 | async-start | bytes 4718592 | tf_op jit(solution)/shard_map/reduce_scatter | solution.py:46
  193.7 4.9 %copy-start.3 = (f32[1,384]{1,0:T(1,128)S(1)}, f32[1,384]{1,0:T(1,128)}, u32[]{:S(2)}) copy-start(f32[1,384]{1,0:T(1,128)} %param.12) | copy-start | bytes 4612
  193.7 45.3 %all-to-all-start.1 = ((bf16[16,72,768]{2,1,0:T(8,128)(2,1)}), bf16[16,72,768]{2,1,0:T(8,128)(2,1)S(1)}, u32[]{:S(2)}, u32[]{:S(2)}) async-start(bf16[16,72,768]{2,1,0:T(8,128)(2,1)} %bitcast.48), calls=%async_computation.1 | async-start | bytes 3538944 | tf_op jit(solution)/shard_map/all_to_all | solution.py:54
  239.0 7.1 %copy-start.2 = (f32[1,1,2048]{2,1,0:T(1,128)S(1)}, f32[1,1,2048]{2,1,0:T(1,128)}, u32[]{:S(2)}) copy-start(f32[1,1,2048]{2,1,0:T(1,128)} %param.13) | copy-start | bytes 24580
Sparse Core Ops, SparseCore 0:
  75.0 44.4 all-gather.2
  185.3 41.7 reduce-scatter.1
where the time goes:
time: 259 us
  waiting for transfers between devices  174 us (67%)
  other arithmetic  22.2 us (9%)
  matrix products  17.3 us (7%)
  starting transfers between devices  16.6 us (6%)
  between operations  14.8 us (6%)
  local copies, waits for them, and re-layouts  13.4 us (5%)
    all_to_all x1, waiting for transfers between devices, local(): lax.all_to_all(send_scaled, 'ep', split_axis=0, concat_axis=0, tiled=True)  103 us
    all_to_all x1, waiting for transfers between devices, local(): lax.all_to_all(input_grad, 'ep', split_axis=0, concat_axis=0, tiled=True)  40.4 us
    all_to_all x1, waiting for transfers between devices, local(): lax.all_to_all(send_hidden, 'ep', split_axis=0, concat_axis=0, tiled=True)  30.4 us
    scatter x1, other arithmetic, local(): jnp.zeros((slots, width), jnp.bfloat16).at[position].set(scaled)  9.76 us
    dot_general x1, matrix products, local(): lax.dot_general(recv_hidden, recv_scaled, (((0,), (0,)), ((), ())), prefe...  8.83 us
    dot_general x1, matrix products, local(): lax.dot_general(recv_scaled, lax.all_gather(own_block, 'rep', axis=0, til...  8.44 us
    all_to_all x1, starting transfers between devices, local(): lax.all_to_all(send_hidden, 'ep', split_axis=0, concat_axis=0, tiled=True)  6.65 us
    scatter x1, local copies, waits for them, and re-layouts, local(): jnp.zeros((slots, inner), jnp.bfloat16).at[position]  6.55 us
  transfers between devices with their start and end apart: 5, of which 3 were waited for; matrix products, arithmetic and copies ran while one was open for 13% of the time, Pallas kernels for 0%

commit v1 on v0

--- a/solution.py
+++ b/solution.py
@@ -2,9 +2,47 @@
 import jax.numpy as jnp
 from jax import lax
 from jax.sharding import PartitionSpec as P
+from jax.lax import axis_index, axis_size, ppermute
 
 decay_rate = 0.9
 epsilon = 1e-06
+
+
+def guide_the_plane(piece_in, d_out, array_in):
+    val = piece_in.shape
+    current_arr = jnp.moveaxis(
+        piece_in.reshape(*val[:d_out], array_in, val[d_out] // array_in, *val[d_out + 1 :]),
+        d_out,
+        0,
+    )
+    return current_arr
+
+
+def test_scales(unit, in_dim):
+    unit = jnp.moveaxis(unit, 0, in_dim)
+    aux = unit.shape
+    r1 = unit.reshape(*aux[:in_dim], aux[in_dim] * aux[in_dim + 1], *aux[in_dim + 2 :])
+    return r1
+
+
+def test_the_positions(point, bus_axis, arr, patch):
+    m_next = axis_size(bus_axis)
+    next_value, e_now = (m_next, axis_index(bus_axis))
+    mid_arr = guide_the_plane(point, arr, next_value)
+    by_place = [mid_arr[e_now]]
+    for j0 in range(1, next_value):
+        extra = mid_arr[(e_now + j0) % next_value]
+        by_place.append(
+            ppermute(
+                extra,
+                axis_name=bus_axis,
+                perm=[(m, (m + j0) % next_value) for m in range(next_value)],
+            )
+        )
+    far_arr = jnp.stack(by_place, axis=0)
+    mid_arr = far_arr[(e_now - jnp.arange(next_value)) % next_value]
+    block_next = test_scales(mid_arr, patch)
+    return block_next
 
 
 def local(out_grad, hidden, expert_ids, gates, weights, row_moment, col_moment):
@@ -30,7 +68,7 @@
         jnp.zeros((slots, inner), jnp.bfloat16).at[position].set(hidden.reshape(routes, inner))
     )
     recv_scaled, recv_hidden = (
-        lax.all_to_all(send_scaled, "ep", split_axis=0, concat_axis=0, tiled=True),
+        test_the_positions(send_scaled, "ep", 0, 0),
         lax.all_to_all(send_hidden, "ep", split_axis=0, concat_axis=0, tiled=True),
     )
     own_block = weights[0]

time: 259 us -> 271 us (1.046)
  local copies, waits for them, and re-layouts: 13.4 us -> 40.2 us
  waiting for transfers between devices: 174 us -> 152 us
  starting transfers between devices: 16.6 us -> 23.5 us
    ppermute x0 -> x15, waiting for transfers between devices: none -> 111 us  [test_the_positions(): ppermute(extra, axis_name=bus_axis, perm=[(m, (m + j0) % next_value) for...]
    all_to_all x1 -> x0, waiting for transfers between devices: 103 us -> none  [local(): lax.all_to_all(send_scaled, 'ep', split_axis=0, concat_axis=0, tiled=True)]
    all_to_all x1, waiting for transfers between devices: 30.4 us -> 0.01 us  [local(): lax.all_to_all(send_hidden, 'ep', split_axis=0, concat_axis=0, tiled=True)]
    unnamed x12 -> x26, local copies, waits for them, and re-layouts: 0.91 us -> 16.9 us
    ppermute x0 -> x15, starting transfers between devices: none -> 12.9 us  [test_the_positions(): ppermute(extra, axis_name=bus_axis, perm=[(m, (m + j0) % next_value) for...]
    gather x0 -> x1, local copies, waits for them, and re-layouts: none -> 5.44 us  [test_the_positions(): mid_arr = far_arr[(e_now - jnp.arange(next_value)) % next_value]]
    all_to_all x1 -> x0, starting transfers between devices: 4.78 us -> none  [local(): lax.all_to_all(send_scaled, 'ep', split_axis=0, concat_axis=0, tiled=True)]
    squeeze x0 -> x1, local copies, waits for them, and re-layouts: none -> 4.48 us  [test_the_positions(): extra = mid_arr[(e_now + j0) % next_value]]
  transfers between devices with their start and end apart: 5 -> 19, of which waited for: 3 -> 8; matrix products, arithmetic and copies ran while one was open for 13% -> 18% of each run, Pallas kernels for 0% -> 0%
where the time goes in v1:
time: 271 us; the launch traced here: 270 us
  waiting for transfers between devices  152 us (56%)
  local copies, waits for them, and re-layouts  40.2 us (15%)
  starting transfers between devices  23.5 us (9%)
  other arithmetic  23.2 us (9%)
  matrix products  16.5 us (6%)
  between operations  15.1 us (6%)
    ppermute x15, waiting for transfers between devices, test_the_positions(): ppermute(extra, axis_name=bus_axis, perm=[(m, (m + j0) % next_value) for...  111 us
    all_to_all x1, waiting for transfers between devices, local(): lax.all_to_all(input_grad, 'ep', split_axis=0, concat_axis=0, tiled=True)  40.4 us
    unnamed x26, local copies, waits for them, and re-layouts  16.9 us
    ppermute x15, starting transfers between devices, test_the_positions(): ppermute(extra, axis_name=bus_axis, perm=[(m, (m + j0) % next_value) for...  12.9 us
    scatter x1, other arithmetic, local(): jnp.zeros((slots, width), jnp.bfloat16).at[position].set(scaled)  9.77 us
    dot_general x1, matrix products, local(): lax.dot_general(recv_scaled, lax.all_gather(own_block, 'rep', axis=0, til...  8.5 us
    dot_general x1, matrix products, local(): lax.dot_general(recv_hidden, recv_scaled, (((0,), (0,)), ((), ())), prefe...  8 us
    scatter x1, local copies, waits for them, and re-layouts, local(): jnp.zeros((slots, inner), jnp.bfloat16).at[position]  6.63 us
  transfers between devices with their start and end apart: 19, of which 8 were waited for; matrix products, arithmetic and copies ran while one was open for 18% of the time, Pallas kernels for 0%

profile of v1, /device:TPU:15, one launch (start us, length us, event | category | flops | bytes accessed | tf_op | source)
XLA Modules:
  0.0 270.2 jit_solution(902013043762925146)
XLA Ops:
  7.4 0.9 copy.14
  8.3 0.1 eq.47
  8.4 0.1 eq.43
  8.4 0.7 broadcast_multiply_fusion.1
  9.1 4.5 %reduce-window.6 = s32[16,8,128]{2,1,0:T(8,128)S(1)} reduce-window(s32[16,8,128]{2,1,0:T(8,128)S(1)} %fusion.17, s32[]{:T(128)} %constant.120.clone.1), window={size=1x1x128 pad=0_0x0_0x127_0}, to_apply=%region_0.0 | reduce-window | flops 2080768 | bytes 131076 | tf_op jit(solution)/shard_map/reduce-window
  13.7 0.1 slice.12
  13.7 0.1 copy.16
  13.9 0.1 copy.17
  14.0 0.1 broadcast_add_fusion
  14.1 0.1 copy.13
  14.2 0.1 mul.126
  14.3 1.1 convert_element_type.31
  15.4 0.8 copy.18
  16.2 0.1 mul.128
  16.4 9.8 %scatter_custom_fusion = bf16[1152,2048]{1,0:T(8,128)(2,1)} fusion(s32[1024]{0:T(1024)S(1)} %bitcast.118, f32[128,2048]{1,0:T(8,128)S(1)} %convert_element_type.31, f32[1024]{0:T(1024)S(1)} %mul.128, bf16[]{:T(256)} %constant.118.clone.1), kind=kCustom, calls=%fused_computation.7 | custom fusion | flops 4194304 | bytes 5771266 | tf_op jit(solution)/shard_map/scatter | solution.py:66
  26.2 4.5 %dynamic-slice_bitcast_fusion = (bf16[72,2048]{1,0:T(8,128)(2,1)}, bf16[72,2048]{1,0:T(8,128)(2,1)}, bf16[72,2048]{1,0:T(8,128)(2,1)}, bf16[72,2048]{1,0:T(8,128...) fusion(bf16[16,72,2048]{2,1,0:T(8,128)(2,1)} %bitcast.109, ...), kind=kLoop, calls=%fused_computation.37 | loop fusion | bytes 9437248 | tf_op jit(solution)/shard_map/squeeze | solution.py:34
  30.7 1.9 collective-permute-start
  32.5 1.2 collective-permute-start.1
  33.8 0.4 collective-permute-start.2
  34.2 0.9 collective-permute-start.3
  35.1 2.7 collective-permute-start.4
  37.8 6.6 %scatter_custom_fusion.1 = bf16[1152,768]{1,0:T(8,128)(2,1)} fusion(s32[1024]{0:T(1024)S(1)} %bitcast.119, bf16[128,8,768]{2,1,0:T(8,128)(2,1)S(1)} %copy-done, bf16[]{:T(256)} %constant.118.clone.1), kind=kCustom, calls=%fused_computation.19 | custom fusion | bytes 3342338 | tf_op jit(solution)/shard_map/scatter | solution.py:68
  44.4 5.1 %all-to-all-start.1 = ((bf16[16,72,768]{2,1,0:T(8,128)(2,1)}), bf16[16,72,768]{2,1,0:T(8,128)(2,1)S(1)}, u32[]{:S(2)}, u32[]{:S(2)}) async-start(bf16[16,72,768]{2,1,0:T(8,128)(2,1)} %bitcast.43), calls=%async_computation.1 | async-start | bytes 3538944 | tf_op jit(solution)/shard_map/all_to_all | solution.py:72
  49.5 0.0 all-gather.3.cloned.1.call-start
  49.5 0.7 all-gather.3.cloned.1.call-update
  50.2 0.0 reduce-scatter.2.cloned.1.call-start
  50.3 2.1 collective-permute-start.5
  52.5 1.7 bitcast_dynamic-update-slice_fusion.14
  54.2 0.8 collective-permute-start.6
  55.0 1.7 bitcast_dynamic-update-slice_fusion.13
  56.7 2.1 collective-permute-start.7
  58.8 1.7 bitcast_dynamic-update-slice_fusion.12
  60.5 0.3 collective-permute-start.8
  60.8 1.8 bitcast_dynamic-update-slice_fusion.11
  62.6 15.0 %collective-permute-done.4 = bf16[72,2048]{1,0:T(8,128)(2,1)} collective-permute-done((bf16[72,2048]{1,0:T(8,128)(2,1)}, bf16[72,2048]{1,0:T(8,128)(2,1)}, u32[]{:S(2)}, u32[]{:S(2)}) %collective-permute-start.4) | collective-permute-done | bytes 294944 | tf_op jit(solution)/shard_map/ppermute | solution.py:36
  77.6 1.7 bitcast_dynamic-update-slice_fusion.10
  79.3 70.3 %collective-permute-done.5 = bf16[72,2048]{1,0:T(8,128)(2,1)S(1)} collective-permute-done((bf16[72,2048]{1,0:T(8,128)(2,1)}, bf16[72,2048]{1,0:T(8,128)(2,1)S(1)}, u32[]{:S(2)}, u32[]{:S(2)}) %collective-permute-start.5) | collective-permute-done | bytes 294944 | tf_op jit(solution)/shard_map/ppermute | solution.py:36
  149.6 0.7 bitcast_dynamic-update-slice_fusion.9
  150.4 5.7 %collective-permute-done.6 = bf16[72,2048]{1,0:T(8,128)(2,1)S(1)} collective-permute-done((bf16[72,2048]{1,0:T(8,128)(2,1)}, bf16[72,2048]{1,0:T(8,128)(2,1)S(1)}, u32[]{:S(2)}, u32[]{:S(2)}) %collective-permute-start.6) | collective-permute-done | bytes 294944 | tf_op jit(solution)/shard_map/ppermute | solution.py:36
  156.0 0.7 bitcast_dynamic-update-slice_fusion.8
  156.8 11.7 %collective-permute-done.7 = bf16[72,2048]{1,0:T(8,128)(2,1)S(1)} collective-permute-done((bf16[72,2048]{1,0:T(8,128)(2,1)}, bf16[72,2048]{1,0:T(8,128)(2,1)S(1)}, u32[]{:S(2)}, u32[]{:S(2)}) %collective-permute-start.7) | collective-permute-done | bytes 294944 | tf_op jit(solution)/shard_map/ppermute | solution.py:36
  168.5 0.7 bitcast_dynamic-update-slice_fusion.7
  169.2 0.7 bitcast_dynamic-update-slice_fusion.6
  170.0 0.4 collective-permute-start.14
  170.4 0.8 bitcast_dynamic-update-slice_fusion.5
  171.2 0.7 bitcast_dynamic-update-slice_fusion.4
  171.9 0.7 bitcast_dynamic-update-slice_fusion.3
  172.6 2.5 collective-permute-done.12
  175.1 0.7 bitcast_dynamic-update-slice_fusion.2
  175.9 4.8 %collective-permute-done.13 = bf16[72,2048]{1,0:T(8,128)(2,1)S(1)} collective-permute-done((bf16[72,2048]{1,0:T(8,128)(2,1)S(1)}, bf16[72,2048]{1,0:T(8,128)(2,1)S(1)}, u32[]{:S(2)}, u32[]{:S(2)}) %collective-permute-start.13) | collective-permute-done | bytes 294944 | tf_op jit(solution)/shard_map/ppermute | solution.py:36
  180.7 0.7 bitcast_dynamic-update-slice_fusion.1
  181.4 0.6 collective-permute-done.14
  182.0 0.8 bitcast_dynamic-update-slice_fusion
  182.7 5.4 %gather_fusion = bf16[16,72,2048]{2,1,0:T(8,128)(2,1)} fusion(bf16[16,72,2048]{2,1,0:T(8,128)(2,1)} %bitcast_dynamic-update-slice_fusion, s32[1024]{0:T(1024)S(1)} %pad_clamp_fusion), kind=kCustom, calls=%fused_computation | custom fusion | bytes 9437248 | tf_op jit(solution)/shard_map/gather | solution.py:43
  188.2 8.0 %bitcast_convert_fusion = bf16[768,2048]{1,0:T(8,128)(2,1)} fusion(bf16[16,72,768]{2,1,0:T(8,128)(2,1)S(1)} %all-to-all-done.1, bf16[16,72,2048]{2,1,0:T(8,128)(2,1)} %gather_fusion), kind=kOutput, calls=%fused_computation.6 | convolution fusion | flops 3625451520 | bytes 9633792 | tf_op jit(solution)/shard_map/dot_general | solution.py:81
  196.3 8.5 %convolution_convert_fusion = bf16[1152,768]{1,0:T(8,128)(2,1)} fusion(bf16[1152,2048]{1,0:T(8,128)(2,1)} %bitcast.110, bf16[1,768,2048]{2,1,0:T(8,128)(2,1)} %all-gather.3.cloned.1.call-done), kind=kOutput, calls=%fused_computation.14 | convolution fusion | flops 3624763392 | bytes 9633792 | tf_op jit(solution)/shard_map/dot_general | solution.py:75
  204.8 5.4 %all-to-all-start = ((bf16[16,72,768]{2,1,0:T(8,128)(2,1)}), bf16[16,72,768]{2,1,0:T(8,128)(2,1)S(1)}, u32[]{:S(2)}, u32[]{:S(2)}) async-start(bf16[16,72,768]{2,1,0:T(8,128)(2,1)} %bitcast.111), calls=%async_computation | async-start | bytes 3538944 | tf_op jit(solution)/shard_map/all_to_all | solution.py:92
  210.2 40.4 %all-to-all-done = bf16[16,72,768]{2,1,0:T(8,128)(2,1)S(1)} async-done(((bf16[16,72,768]{2,1,0:T(8,128)(2,1)}), bf16[16,72,768]{2,1,0:T(8,128)(2,1)S(1)}, u32[]{:S(2)}, u32[]{:S(2)}) %all-to-all-start) | async-done | bytes 1769504 | tf_op jit(solution)/shard_map/all_to_all | solution.py:92
  250.6 5.2 %gather_fusion.1 = bf16[1024,768]{1,0:T(8,128)(2,1)} fusion(bf16[1152,768]{1,0:T(8,128)(2,1)S(1)} %bitcast.108, s32[1024]{0:T(1024)S(1)} %broadcast_clamp_fusion), kind=kCustom, calls=%fused_computation.1 | custom fusion | bytes 3149824 | tf_op jit(solution)/shard_map/gather | solution.py:93
  255.8 1.9 fusion.5
  257.7 0.6 fusion.22
  258.3 0.6 fusion.23
  258.9 0.6 reshape_add_fusion
  260.1 3.2 %fusion.10 = bf16[1,384,2048]{2,1,0:T(8,128)(2,1)} fusion(bf16[384,2048]{1,0:T(8,128)(2,1)} %reduce-scatter.2.cloned.1.call-done, f32[]{:T(128)S(6)} %div.25, f32[2048]{0:T(1024)S(1)} %fusion.21, f32[384]{0:T(512)S(1)} %get-tuple-element.7), kind=kLoop, calls=%fused_computation.18 | loop fusion | flops 3932160 | bytes 3155460 | tf_op jit(solution)/shard_map/broadcast_in_dim | solution.py:103
  (38 shorter events, 0.2 us)
Async XLA Ops:
  7.2 30.6 %copy-start = (bf16[128,8,768]{2,1,0:T(8,128)(2,1)S(1)}, bf16[128,8,768]{2,1,0:T(8,128)(2,1)}, u32[]{:S(2)}) copy-start(bf16[128,8,768]{2,1,0:T(8,128)(2,1)} %param.8) | copy-start | bytes 4718596
  30.7 19.6 %collective-permute-start = (bf16[72,2048]{1,0:T(8,128)(2,1)}, bf16[72,2048]{1,0:T(8,128)(2,1)}, u32[]{:S(2)}, u32[]{:S(2)}) collective-permute-start(bf16[72,2048]{1,0:T(8,128)(2,1)} %get-tuple-element.22), channel_id=1, source_target_pairs={{0,2},{2,4},{4,6},{6,8},{8,10},{10,12},{12,14},{14,16},{16,18},{18... | collective-permute-start | bytes 884744 | tf_op jit(solution)/shard_map/ppermute | solution.py:36
  32.5 21.6 %collective-permute-start.1 = (bf16[72,2048]{1,0:T(8,128)(2,1)}, bf16[72,2048]{1,0:T(8,128)(2,1)}, u32[]{:S(2)}, u32[]{:S(2)}) collective-permute-start(bf16[72,2048]{1,0:T(8,128)(2,1)} %get-tuple-element.21), channel_id=1, source_target_pairs={{0,4},{2,6},{4,8},{6,10},{8,12},{10,14},{12,16},{14,18},{16,20},{1... | collective-permute-start | bytes 884744 | tf_op jit(solution)/shard_map/ppermute | solution.py:36
  33.8 22.9 %collective-permute-start.2 = (bf16[72,2048]{1,0:T(8,128)(2,1)}, bf16[72,2048]{1,0:T(8,128)(2,1)}, u32[]{:S(2)}, u32[]{:S(2)}) collective-permute-start(bf16[72,2048]{1,0:T(8,128)(2,1)} %get-tuple-element.20), channel_id=1, source_target_pairs={{0,6},{2,8},{4,10},{6,12},{8,14},{10,16},{12,18},{14,20},{16,22},{... | collective-permute-start | bytes 884744 | tf_op jit(solution)/shard_map/ppermute | solution.py:36
  34.2 26.3 %collective-permute-start.3 = (bf16[72,2048]{1,0:T(8,128)(2,1)}, bf16[72,2048]{1,0:T(8,128)(2,1)}, u32[]{:S(2)}, u32[]{:S(2)}) collective-permute-start(bf16[72,2048]{1,0:T(8,128)(2,1)} %get-tuple-element.19), channel_id=1, source_target_pairs={{0,8},{2,10},{4,12},{6,14},{8,16},{10,18},{12,20},{14,22},{16,24},... | collective-permute-start | bytes 884744 | tf_op jit(solution)/shard_map/ppermute | solution.py:36
  35.1 42.5 %collective-permute-start.4 = (bf16[72,2048]{1,0:T(8,128)(2,1)}, bf16[72,2048]{1,0:T(8,128)(2,1)}, u32[]{:S(2)}, u32[]{:S(2)}) collective-permute-start(bf16[72,2048]{1,0:T(8,128)(2,1)} %get-tuple-element.18), channel_id=1, source_target_pairs={{0,10},{2,12},{4,14},{6,16},{8,18},{10,20},{12,22},{14,24},{16,26}... | collective-permute-start | bytes 884744 | tf_op jit(solution)/shard_map/ppermute | solution.py:36
  44.4 143.8 %all-to-all-start.1 = ((bf16[16,72,768]{2,1,0:T(8,128)(2,1)}), bf16[16,72,768]{2,1,0:T(8,128)(2,1)S(1)}, u32[]{:S(2)}, u32[]{:S(2)}) async-start(bf16[16,72,768]{2,1,0:T(8,128)(2,1)} %bitcast.43), calls=%async_computation.1 | async-start | bytes 3538944 | tf_op jit(solution)/shard_map/all_to_all | solution.py:72
  49.5 146.7 %all-gather.3.cloned.1.call-start = ((), (), s32[]{:S(2)}) async-start(), calls=%async_computation.4 | async-start | bytes 4718592 | tf_op jit(solution)/shard_map/all_gather | solution.py:77
  50.2 205.6 %reduce-scatter.2.cloned.1.call-start = ((), (), s32[]{:S(2)}) async-start(), calls=%async_computation.3 | async-start | bytes 4718592 | tf_op jit(solution)/shard_map/reduce_scatter | solution.py:84
  50.3 118.9 %copy-start.2 = (bf16[72,2048]{1,0:T(8,128)(2,1)S(1)}, bf16[72,2048]{1,0:T(8,128)(2,1)}, u32[]{:S(2)}) copy-start(bf16[72,2048]{1,0:T(8,128)(2,1)} %get-tuple-element.9) | copy-start | bytes 884740
  50.3 119.7 %copy-start.1 = (bf16[72,2048]{1,0:T(8,128)(2,1)S(1)}, bf16[72,2048]{1,0:T(8,128)(2,1)}, u32[]{:S(2)}) copy-start(bf16[72,2048]{1,0:T(8,128)(2,1)} %get-tuple-element.8) | copy-start | bytes 884740
  50.3 99.3 %collective-permute-start.5 = (bf16[72,2048]{1,0:T(8,128)(2,1)}, bf16[72,2048]{1,0:T(8,128)(2,1)S(1)}, u32[]{:S(2)}, u32[]{:S(2)}) collective-permute-start(bf16[72,2048]{1,0:T(8,128)(2,1)} %get-tuple-element.17), channel_id=1, source_target_pairs={{0,12},{2,14},{4,16},{6,18},{8,20},{10,22},{12,24},{14,26},{16,28}... | collective-permute-start | bytes 884744 | tf_op jit(solution)/shard_map/ppermute | solution.py:36
  54.2 101.9 %collective-permute-start.6 = (bf16[72,2048]{1,0:T(8,128)(2,1)}, bf16[72,2048]{1,0:T(8,128)(2,1)S(1)}, u32[]{:S(2)}, u32[]{:S(2)}) collective-permute-start(bf16[72,2048]{1,0:T(8,128)(2,1)} %get-tuple-element.16), channel_id=1, source_target_pairs={{0,14},{2,16},{4,18},{6,20},{8,22},{10,24},{12,26},{14,28},{16,30}... | collective-permute-start | bytes 884744 | tf_op jit(solution)/shard_map/ppermute | solution.py:36
  56.7 111.8 %collective-permute-start.7 = (bf16[72,2048]{1,0:T(8,128)(2,1)}, bf16[72,2048]{1,0:T(8,128)(2,1)S(1)}, u32[]{:S(2)}, u32[]{:S(2)}) collective-permute-start(bf16[72,2048]{1,0:T(8,128)(2,1)} %get-tuple-element.15), channel_id=1, source_target_pairs={{0,16},{2,18},{4,20},{6,22},{8,24},{10,26},{12,28},{14,30},{16,0},... | collective-permute-start | bytes 884744 | tf_op jit(solution)/shard_map/ppermute | solution.py:36
  60.5 108.7 %collective-permute-start.8 = (bf16[72,2048]{1,0:T(8,128)(2,1)}, bf16[72,2048]{1,0:T(8,128)(2,1)S(1)}, u32[]{:S(2)}, u32[]{:S(2)}) collective-permute-start(bf16[72,2048]{1,0:T(8,128)(2,1)} %get-tuple-element.14), channel_id=1, source_target_pairs={{0,18},{2,20},{4,22},{6,24},{8,26},{10,28},{12,30},{14,0},{16,2},{... | collective-permute-start | bytes 884744 | tf_op jit(solution)/shard_map/ppermute | solution.py:36
  77.6 92.3 %collective-permute-start.9 = (bf16[72,2048]{1,0:T(8,128)(2,1)}, bf16[72,2048]{1,0:T(8,128)(2,1)S(1)}, u32[]{:S(2)}, u32[]{:S(2)}) collective-permute-start(bf16[72,2048]{1,0:T(8,128)(2,1)} %get-tuple-element.13), channel_id=1, source_target_pairs={{0,20},{2,22},{4,24},{6,26},{8,28},{10,30},{12,0},{14,2},{16,4},{1... | collective-permute-start | bytes 884744 | tf_op jit(solution)/shard_map/ppermute | solution.py:36
  149.6 21.5 %collective-permute-start.10 = (bf16[72,2048]{1,0:T(8,128)(2,1)}, bf16[72,2048]{1,0:T(8,128)(2,1)S(1)}, u32[]{:S(2)}, u32[]{:S(2)}) collective-permute-start(bf16[72,2048]{1,0:T(8,128)(2,1)} %get-tuple-element.12), channel_id=1, source_target_pairs={{0,22},{2,24},{4,26},{6,28},{8,30},{10,0},{12,2},{14,4},{16,6},{18... | collective-permute-start | bytes 884744 | tf_op jit(solution)/shard_map/ppermute | solution.py:36
  156.0 15.9 %collective-permute-start.11 = (bf16[72,2048]{1,0:T(8,128)(2,1)}, bf16[72,2048]{1,0:T(8,128)(2,1)S(1)}, u32[]{:S(2)}, u32[]{:S(2)}) collective-permute-start(bf16[72,2048]{1,0:T(8,128)(2,1)} %get-tuple-element.11), channel_id=1, source_target_pairs={{0,24},{2,26},{4,28},{6,30},{8,0},{10,2},{12,4},{14,6},{16,8},{18,... | collective-permute-start | bytes 884744 | tf_op jit(solution)/shard_map/ppermute | solution.py:36
  168.5 6.7 %collective-permute-start.12 = (bf16[72,2048]{1,0:T(8,128)(2,1)}, bf16[72,2048]{1,0:T(8,128)(2,1)S(1)}, u32[]{:S(2)}, u32[]{:S(2)}) collective-permute-start(bf16[72,2048]{1,0:T(8,128)(2,1)} %get-tuple-element.10), channel_id=1, source_target_pairs={{0,26},{2,28},{4,30},{6,0},{8,2},{10,4},{12,6},{14,8},{16,10},{18,... | collective-permute-start | bytes 884744 | tf_op jit(solution)/shard_map/ppermute | solution.py:36
  169.2 11.5 %collective-permute-start.13 = (bf16[72,2048]{1,0:T(8,128)(2,1)S(1)}, bf16[72,2048]{1,0:T(8,128)(2,1)S(1)}, u32[]{:S(2)}, u32[]{:S(2)}) collective-permute-start(bf16[72,2048]{1,0:T(8,128)(2,1)S(1)} %copy-done.2), channel_id=1, source_target_pairs={{0,28},{2,30},{4,0},{6,2},{8,4},{10,6},{12,8},{14,10},{16,12},{18,... | collective-permute-start | bytes 884744 | tf_op jit(solution)/shard_map/ppermute | solution.py:36
  170.0 12.0 %collective-permute-start.14 = (bf16[72,2048]{1,0:T(8,128)(2,1)S(1)}, bf16[72,2048]{1,0:T(8,128)(2,1)S(1)}, u32[]{:S(2)}, u32[]{:S(2)}) collective-permute-start(bf16[72,2048]{1,0:T(8,128)(2,1)S(1)} %copy-done.1), channel_id=1, source_target_pairs={{0,30},{2,0},{4,2},{6,4},{8,6},{10,8},{12,10},{14,12},{16,14},{18,... | collective-permute-start | bytes 884744 | tf_op jit(solution)/shard_map/ppermute | solution.py:36
  196.2 13.9 %copy-start.4 = (f32[1,384]{1,0:T(1,128)S(1)}, f32[1,384]{1,0:T(1,128)}, u32[]{:S(2)}) copy-start(f32[1,384]{1,0:T(1,128)} %param.12) | copy-start | bytes 4612
  204.8 45.8 %all-to-all-start = ((bf16[16,72,768]{2,1,0:T(8,128)(2,1)}), bf16[16,72,768]{2,1,0:T(8,128)(2,1)S(1)}, u32[]{:S(2)}, u32[]{:S(2)}) async-start(bf16[16,72,768]{2,1,0:T(8,128)(2,1)} %bitcast.111), calls=%async_computation | async-start | bytes 3538944 | tf_op jit(solution)/shard_map/all_to_all | solution.py:92
  250.6 7.1 %copy-start.3 = (f32[1,1,2048]{2,1,0:T(1,128)S(1)}, f32[1,1,2048]{2,1,0:T(1,128)}, u32[]{:S(2)}) copy-start(f32[1,1,2048]{2,1,0:T(1,128)} %param.13) | copy-start | bytes 24580
Sparse Core Ops, SparseCore 0:
  51.8 44.4 all-gather.2
  196.3 42.3 reduce-scatter.1
